TPU v7x, 32 devices: a whole 2x2x4 slice. The times are simulated.
32 devices in a mesh: groups: 2 (over x), tok: 16 (over z, y, core).
Axes of the slice: x: 2, y: 2, z: 4, core: 2. Of those that a mesh axis runs over, the one named last changes fastest.
Arguments:
- activations: bfloat16 [8, 4096, 128], P(None, ('groups', 'tok')), parts along dimension 1, may hold values from -1.796875 to 1.796875
- gradients: bfloat16 [8, 4096, 128], P(None, ('groups', 'tok')), parts along dimension 1, may hold values from -1.796875 to 1.796875
- queries: bfloat16 [64, 4096], P(None, ('groups', 'tok')), parts along dimension 1, may hold values from -0.125 to 0.125
- layer_ids: int32 [3], replicated, may hold values from 0 to 7
Outputs:
- influence: float32 [64, 4096], P(None, ('groups', 'tok')), parts along dimension 1
There are 2 independent parts, one for each index of `groups`. A program takes and returns all parts, laid end to end along the dimension named above; an argument that names none is the same for every part. Nothing has to cross between parts.
Inputs may be any that keep to these rules, and one draw needn't show every extreme that they name: `layer_ids`: indices of stored layers; they may repeat.
All inputs are finite; a program needn't handle non-finite values.
Results may differ from a plain program's by a relative error of at most 0.0029.
Values may be sent and summed in bfloat16 or wider, within the bound.
A program may use at most 64 MiB of HBM per device.

v0:
```python
import jax
import jax.numpy as jnp
from jax import lax
from jax.sharding import PartitionSpec as P


def passed_along(block, axis, distance):
    devices = range(lax.axis_size(axis))
    route = [((i - distance) % len(devices), i) for i in devices]
    return lax.ppermute(block, axis, route)


def token_pair_function(local_token_block, passing_block):
    input_product_matrix = jnp.einsum(
        "qun,qpn->qup", local_token_block[0], passing_block[0], preferred_element_type=jnp.float32
    )
    grad_gram = jnp.einsum(
        "qun,qpn->qup", local_token_block[1], passing_block[1], preferred_element_type=jnp.float32
    )
    return jnp.sum(input_product_matrix * grad_gram, axis=0).astype(jnp.bfloat16)


def rows_term(kernel, visitor_queries):
    return lax.dot_general(
        visitor_queries, kernel, (((1,), (1,)), ((), ())), preferred_element_type=jnp.float32
    )


def body(activations, gradients, queries, layer_ids):
    local_token_block = jnp.stack(
        [jnp.take(activations, layer_ids, axis=0), jnp.take(gradients, layer_ids, axis=0)]
    )
    half_cycle = lax.axis_size("tok") // 2
    influence = rows_term(token_pair_function(local_token_block, local_token_block), queries)

    def upward(stream):
        return passed_along((stream[0], stream[1]), "tok", -1)

    def downward(stream):
        return passed_along((stream[0], stream[1]), "tok", 1)

    def turn(turn_index, carried_state):
        result, rising_block_payload, downward_data = carried_state
        rising_block_payload = upward(rising_block_payload)
        downward_data = downward(downward_data)
        result = result + rows_term(
            token_pair_function(local_token_block, rising_block_payload[0]), rising_block_payload[1]
        )
        result = result + rows_term(
            token_pair_function(local_token_block, downward_data[0]), downward_data[1]
        )
        return (result, rising_block_payload, downward_data)

    initial = (influence, (local_token_block, queries), (local_token_block, queries))
    influence, rising_block_payload, downward_data = lax.fori_loop(0, half_cycle - 1, turn, initial)
    rising_block_payload = upward(rising_block_payload)
    influence = influence + rows_term(
        token_pair_function(local_token_block, rising_block_payload[0]), rising_block_payload[1]
    )
    return influence


def solution(mesh):
    return jax.shard_map(
        body,
        mesh=mesh,
        in_specs=(
            P(None, ("groups", "tok"), None),
            P(None, ("groups", "tok"), None),
            P(None, ("groups", "tok")),
            P(),
        ),
        out_specs=P(None, ("groups", "tok")),
        check_vma=False,
    )
```

profile of v0, /device:TPU:0, one launch (start us, length us, event | category | flops | bytes accessed | tf_op | source)
XLA Modules:
  0.0 78.9 jit_solution(1737522119606937563)
XLA Ops:
  0.0 0.8 copy.25
  1.6 1.5 %gather_fusion.1 = bf16[3,128,128]{2,1,0:T(8,128)(2,1)S(1)} fusion(bf16[8,128,128]{2,1,0:T(8,128)(2,1)} %param.9, s32[1024]{0:T(1024)S(1)} %pad_clamp_fusion), kind=kCustom, calls=%fused_computation.1.clone | custom fusion | bytes 196620 | tf_op jit(solution)/shard_map/jit(_take)/gather | solution.py:31
  3.8 70.7 %while.18 = (s32[]{:T(128)}, f32[64,128]{1,0:T(8,128)S(1)}, bf16[2,3,128,128]{3,2,1,0:T(8,128)(2,1)S(1)}, bf16[64,128]{1,0:T(8,128)(2,1)S(1)}, bf16[2,3,128,128]...) while((s32[]{:T(128)}, f32[64,128]{1,0:T(8,128)S(1)}, ...), condition=%wide.region_4.0_spmd, body=%wide.region_1.5_spmd.sunk | while | flops 54706176 | bytes 4423933 | solution.py:55
  3.8 5.5 %collective-permute-start.3 = (bf16[2,3,128,128]{3,2,1,0:T(8,128)(2,1)S(1)}, bf16[2,3,128,128]{3,2,1,0:T(8,128)(2,1)S(1)}, u32[]{:S(2)}, u32[]{:S(2)}) collective-permute-start(bf16[2,3,128,128]{3,2,1,0:T(8,128)(2,1)S(1)} %get-tuple-element.131), channel_id=1, source_target_pairs={{1,0},{2,1},{3,2},{4,3},{5,4},{6,5},{7,6},{8,7},{9,8},{10,9},{11,1... | collective-permute-start | bytes 589832 | tf_op jit(solution)/shard_map/while/body/eval_jaxpr/ppermute | solution.py:10
  10.0 2.7 %collective-permute-done.2 = bf16[64,128]{1,0:T(8,128)(2,1)S(1)} collective-permute-done((bf16[64,128]{1,0:T(8,128)(2,1)S(1)}, bf16[64,128]{1,0:T(8,128)(2,1)S(1)}, u32[]{:S(2)}, u32[]{:S(2)}) %collective-permute-start.2) | collective-permute-done | bytes 16416 | tf_op jit(solution)/shard_map/while/body/eval_jaxpr/ppermute | solution.py:10
  12.7 3.2 %collective-permute-done = bf16[64,128]{1,0:T(8,128)(2,1)S(1)} collective-permute-done((bf16[64,128]{1,0:T(8,128)(2,1)S(1)}, bf16[64,128]{1,0:T(8,128)(2,1)S(1)}, u32[]{:S(2)}, u32[]{:S(2)}) %collective-permute-start) | collective-permute-done | bytes 16416 | tf_op jit(solution)/shard_map/while/body/eval_jaxpr/ppermute | solution.py:10
  16.1 1.9 %collective-permute-done.1 = bf16[2,3,128,128]{3,2,1,0:T(8,128)(2,1)S(1)} collective-permute-done((bf16[2,3,128,128]{3,2,1,0:T(8,128)(2,1)S(1)}, bf16[2,3,128,128]{3,2,1,0:T(8,128)(2,1)S(1)}, u32[]{:S(2)}, u32[]{:S(2)}) %collective-permute-start.1) | collective-permute-done | bytes 196640 | tf_op jit(solution)/shard_map/while/body/eval_jaxpr/ppermute | solution.py:10
  19.4 1.7 %collective-permute-start.1 = (bf16[2,3,128,128]{3,2,1,0:T(8,128)(2,1)S(1)}, bf16[2,3,128,128]{3,2,1,0:T(8,128)(2,1)S(1)}, u32[]{:S(2)}, u32[]{:S(2)}) collective-permute-start(bf16[2,3,128,128]{3,2,1,0:T(8,128)(2,1)S(1)} %get-tuple-element.133), channel_id=1, source_target_pairs={{15,0},{0,1},{1,2},{2,3},{3,4},{4,5},{5,6},{6,7},{7,8},{8,9},{9,10... | collective-permute-start | bytes 589832 | tf_op jit(solution)/shard_map/while/body/eval_jaxpr/ppermute | solution.py:10
  21.2 1.1 %collective-permute-done.2 = bf16[64,128]{1,0:T(8,128)(2,1)S(1)} collective-permute-done((bf16[64,128]{1,0:T(8,128)(2,1)S(1)}, bf16[64,128]{1,0:T(8,128)(2,1)S(1)}, u32[]{:S(2)}, u32[]{:S(2)}) %collective-permute-start.2) | collective-permute-done | bytes 16416 | tf_op jit(solution)/shard_map/while/body/eval_jaxpr/ppermute | solution.py:10
  22.3 2.7 %collective-permute-done = bf16[64,128]{1,0:T(8,128)(2,1)S(1)} collective-permute-done((bf16[64,128]{1,0:T(8,128)(2,1)S(1)}, bf16[64,128]{1,0:T(8,128)(2,1)S(1)}, u32[]{:S(2)}, u32[]{:S(2)}) %collective-permute-start) | collective-permute-done | bytes 16416 | tf_op jit(solution)/shard_map/while/body/eval_jaxpr/ppermute | solution.py:10
  25.2 2.1 %collective-permute-done.1 = bf16[2,3,128,128]{3,2,1,0:T(8,128)(2,1)S(1)} collective-permute-done((bf16[2,3,128,128]{3,2,1,0:T(8,128)(2,1)S(1)}, bf16[2,3,128,128]{3,2,1,0:T(8,128)(2,1)S(1)}, u32[]{:S(2)}, u32[]{:S(2)}) %collective-permute-start.1) | collective-permute-done | bytes 196640 | tf_op jit(solution)/shard_map/while/body/eval_jaxpr/ppermute | solution.py:10
  28.7 1.7 %collective-permute-start.1 = (bf16[2,3,128,128]{3,2,1,0:T(8,128)(2,1)S(1)}, bf16[2,3,128,128]{3,2,1,0:T(8,128)(2,1)S(1)}, u32[]{:S(2)}, u32[]{:S(2)}) collective-permute-start(bf16[2,3,128,128]{3,2,1,0:T(8,128)(2,1)S(1)} %get-tuple-element.133), channel_id=1, source_target_pairs={{15,0},{0,1},{1,2},{2,3},{3,4},{4,5},{5,6},{6,7},{7,8},{8,9},{9,10... | collective-permute-start | bytes 589832 | tf_op jit(solution)/shard_map/while/body/eval_jaxpr/ppermute | solution.py:10
  30.4 1.1 %collective-permute-done.2 = bf16[64,128]{1,0:T(8,128)(2,1)S(1)} collective-permute-done((bf16[64,128]{1,0:T(8,128)(2,1)S(1)}, bf16[64,128]{1,0:T(8,128)(2,1)S(1)}, u32[]{:S(2)}, u32[]{:S(2)}) %collective-permute-start.2) | collective-permute-done | bytes 16416 | tf_op jit(solution)/shard_map/while/body/eval_jaxpr/ppermute | solution.py:10
  31.5 2.6 %collective-permute-done = bf16[64,128]{1,0:T(8,128)(2,1)S(1)} collective-permute-done((bf16[64,128]{1,0:T(8,128)(2,1)S(1)}, bf16[64,128]{1,0:T(8,128)(2,1)S(1)}, u32[]{:S(2)}, u32[]{:S(2)}) %collective-permute-start) | collective-permute-done | bytes 16416 | tf_op jit(solution)/shard_map/while/body/eval_jaxpr/ppermute | solution.py:10
  34.3 2.2 %collective-permute-done.1 = bf16[2,3,128,128]{3,2,1,0:T(8,128)(2,1)S(1)} collective-permute-done((bf16[2,3,128,128]{3,2,1,0:T(8,128)(2,1)S(1)}, bf16[2,3,128,128]{3,2,1,0:T(8,128)(2,1)S(1)}, u32[]{:S(2)}, u32[]{:S(2)}) %collective-permute-start.1) | collective-permute-done | bytes 196640 | tf_op jit(solution)/shard_map/while/body/eval_jaxpr/ppermute | solution.py:10
  38.0 1.7 %collective-permute-start.1 = (bf16[2,3,128,128]{3,2,1,0:T(8,128)(2,1)S(1)}, bf16[2,3,128,128]{3,2,1,0:T(8,128)(2,1)S(1)}, u32[]{:S(2)}, u32[]{:S(2)}) collective-permute-start(bf16[2,3,128,128]{3,2,1,0:T(8,128)(2,1)S(1)} %get-tuple-element.133), channel_id=1, source_target_pairs={{15,0},{0,1},{1,2},{2,3},{3,4},{4,5},{5,6},{6,7},{7,8},{8,9},{9,10... | collective-permute-start | bytes 589832 | tf_op jit(solution)/shard_map/while/body/eval_jaxpr/ppermute | solution.py:10
  39.7 1.1 %collective-permute-done.2 = bf16[64,128]{1,0:T(8,128)(2,1)S(1)} collective-permute-done((bf16[64,128]{1,0:T(8,128)(2,1)S(1)}, bf16[64,128]{1,0:T(8,128)(2,1)S(1)}, u32[]{:S(2)}, u32[]{:S(2)}) %collective-permute-start.2) | collective-permute-done | bytes 16416 | tf_op jit(solution)/shard_map/while/body/eval_jaxpr/ppermute | solution.py:10
  40.8 2.6 %collective-permute-done = bf16[64,128]{1,0:T(8,128)(2,1)S(1)} collective-permute-done((bf16[64,128]{1,0:T(8,128)(2,1)S(1)}, bf16[64,128]{1,0:T(8,128)(2,1)S(1)}, u32[]{:S(2)}, u32[]{:S(2)}) %collective-permute-start) | collective-permute-done | bytes 16416 | tf_op jit(solution)/shard_map/while/body/eval_jaxpr/ppermute | solution.py:10
  43.6 2.2 %collective-permute-done.1 = bf16[2,3,128,128]{3,2,1,0:T(8,128)(2,1)S(1)} collective-permute-done((bf16[2,3,128,128]{3,2,1,0:T(8,128)(2,1)S(1)}, bf16[2,3,128,128]{3,2,1,0:T(8,128)(2,1)S(1)}, u32[]{:S(2)}, u32[]{:S(2)}) %collective-permute-start.1) | collective-permute-done | bytes 196640 | tf_op jit(solution)/shard_map/while/body/eval_jaxpr/ppermute | solution.py:10
  47.2 1.7 %collective-permute-start.1 = (bf16[2,3,128,128]{3,2,1,0:T(8,128)(2,1)S(1)}, bf16[2,3,128,128]{3,2,1,0:T(8,128)(2,1)S(1)}, u32[]{:S(2)}, u32[]{:S(2)}) collective-permute-start(bf16[2,3,128,128]{3,2,1,0:T(8,128)(2,1)S(1)} %get-tuple-element.133), channel_id=1, source_target_pairs={{15,0},{0,1},{1,2},{2,3},{3,4},{4,5},{5,6},{6,7},{7,8},{8,9},{9,10... | collective-permute-start | bytes 589832 | tf_op jit(solution)/shard_map/while/body/eval_jaxpr/ppermute | solution.py:10
  49.0 1.1 %collective-permute-done.2 = bf16[64,128]{1,0:T(8,128)(2,1)S(1)} collective-permute-done((bf16[64,128]{1,0:T(8,128)(2,1)S(1)}, bf16[64,128]{1,0:T(8,128)(2,1)S(1)}, u32[]{:S(2)}, u32[]{:S(2)}) %collective-permute-start.2) | collective-permute-done | bytes 16416 | tf_op jit(solution)/shard_map/while/body/eval_jaxpr/ppermute | solution.py:10
  50.1 2.6 %collective-permute-done = bf16[64,128]{1,0:T(8,128)(2,1)S(1)} collective-permute-done((bf16[64,128]{1,0:T(8,128)(2,1)S(1)}, bf16[64,128]{1,0:T(8,128)(2,1)S(1)}, u32[]{:S(2)}, u32[]{:S(2)}) %collective-permute-start) | collective-permute-done | bytes 16416 | tf_op jit(solution)/shard_map/while/body/eval_jaxpr/ppermute | solution.py:10
  52.9 2.2 %collective-permute-done.1 = bf16[2,3,128,128]{3,2,1,0:T(8,128)(2,1)S(1)} collective-permute-done((bf16[2,3,128,128]{3,2,1,0:T(8,128)(2,1)S(1)}, bf16[2,3,128,128]{3,2,1,0:T(8,128)(2,1)S(1)}, u32[]{:S(2)}, u32[]{:S(2)}) %collective-permute-start.1) | collective-permute-done | bytes 196640 | tf_op jit(solution)/shard_map/while/body/eval_jaxpr/ppermute | solution.py:10
  56.5 1.7 %collective-permute-start.1 = (bf16[2,3,128,128]{3,2,1,0:T(8,128)(2,1)S(1)}, bf16[2,3,128,128]{3,2,1,0:T(8,128)(2,1)S(1)}, u32[]{:S(2)}, u32[]{:S(2)}) collective-permute-start(bf16[2,3,128,128]{3,2,1,0:T(8,128)(2,1)S(1)} %get-tuple-element.133), channel_id=1, source_target_pairs={{15,0},{0,1},{1,2},{2,3},{3,4},{4,5},{5,6},{6,7},{7,8},{8,9},{9,10... | collective-permute-start | bytes 589832 | tf_op jit(solution)/shard_map/while/body/eval_jaxpr/ppermute | solution.py:10
  58.2 1.1 %collective-permute-done.2 = bf16[64,128]{1,0:T(8,128)(2,1)S(1)} collective-permute-done((bf16[64,128]{1,0:T(8,128)(2,1)S(1)}, bf16[64,128]{1,0:T(8,128)(2,1)S(1)}, u32[]{:S(2)}, u32[]{:S(2)}) %collective-permute-start.2) | collective-permute-done | bytes 16416 | tf_op jit(solution)/shard_map/while/body/eval_jaxpr/ppermute | solution.py:10
  59.3 2.6 %collective-permute-done = bf16[64,128]{1,0:T(8,128)(2,1)S(1)} collective-permute-done((bf16[64,128]{1,0:T(8,128)(2,1)S(1)}, bf16[64,128]{1,0:T(8,128)(2,1)S(1)}, u32[]{:S(2)}, u32[]{:S(2)}) %collective-permute-start) | collective-permute-done | bytes 16416 | tf_op jit(solution)/shard_map/while/body/eval_jaxpr/ppermute | solution.py:10
  62.1 2.2 %collective-permute-done.1 = bf16[2,3,128,128]{3,2,1,0:T(8,128)(2,1)S(1)} collective-permute-done((bf16[2,3,128,128]{3,2,1,0:T(8,128)(2,1)S(1)}, bf16[2,3,128,128]{3,2,1,0:T(8,128)(2,1)S(1)}, u32[]{:S(2)}, u32[]{:S(2)}) %collective-permute-start.1) | collective-permute-done | bytes 196640 | tf_op jit(solution)/shard_map/while/body/eval_jaxpr/ppermute | solution.py:10
  65.7 1.7 %collective-permute-start.1 = (bf16[2,3,128,128]{3,2,1,0:T(8,128)(2,1)S(1)}, bf16[2,3,128,128]{3,2,1,0:T(8,128)(2,1)S(1)}, u32[]{:S(2)}, u32[]{:S(2)}) collective-permute-start(bf16[2,3,128,128]{3,2,1,0:T(8,128)(2,1)S(1)} %get-tuple-element.133), channel_id=1, source_target_pairs={{15,0},{0,1},{1,2},{2,3},{3,4},{4,5},{5,6},{6,7},{7,8},{8,9},{9,10... | collective-permute-start | bytes 589832 | tf_op jit(solution)/shard_map/while/body/eval_jaxpr/ppermute | solution.py:10
  67.5 1.1 %collective-permute-done.2 = bf16[64,128]{1,0:T(8,128)(2,1)S(1)} collective-permute-done((bf16[64,128]{1,0:T(8,128)(2,1)S(1)}, bf16[64,128]{1,0:T(8,128)(2,1)S(1)}, u32[]{:S(2)}, u32[]{:S(2)}) %collective-permute-start.2) | collective-permute-done | bytes 16416 | tf_op jit(solution)/shard_map/while/body/eval_jaxpr/ppermute | solution.py:10
  68.6 2.6 %collective-permute-done = bf16[64,128]{1,0:T(8,128)(2,1)S(1)} collective-permute-done((bf16[64,128]{1,0:T(8,128)(2,1)S(1)}, bf16[64,128]{1,0:T(8,128)(2,1)S(1)}, u32[]{:S(2)}, u32[]{:S(2)}) %collective-permute-start) | collective-permute-done | bytes 16416 | tf_op jit(solution)/shard_map/while/body/eval_jaxpr/ppermute | solution.py:10
  71.4 2.2 %collective-permute-done.1 = bf16[2,3,128,128]{3,2,1,0:T(8,128)(2,1)S(1)} collective-permute-done((bf16[2,3,128,128]{3,2,1,0:T(8,128)(2,1)S(1)}, bf16[2,3,128,128]{3,2,1,0:T(8,128)(2,1)S(1)}, u32[]{:S(2)}, u32[]{:S(2)}) %collective-permute-start.1) | collective-permute-done | bytes 196640 | tf_op jit(solution)/shard_map/while/body/eval_jaxpr/ppermute | solution.py:10
  74.5 3.2 %collective-permute-done.5 = bf16[2,3,128,128]{3,2,1,0:T(8,128)(2,1)S(1)} collective-permute-done((bf16[2,3,128,128]{3,2,1,0:T(8,128)(2,1)S(1)}, bf16[2,3,128,128]{3,2,1,0:T(8,128)(2,1)S(1)}, u32[]{:S(2)}, u32[]{:S(2)}) %collective-permute-start.5) | collective-permute-done | bytes 196640 | tf_op jit(solution)/shard_map/ppermute | solution.py:10
  (119 shorter events, 14.3 us)
Async XLA Ops:
  0.0 1.0 %copy-start = (bf16[8,128,128]{2,1,0:T(8,128)(2,1)S(1)}, bf16[8,128,128]{2,1,0:T(8,128)(2,1)}, u32[]{:S(2)}) copy-start(bf16[8,128,128]{2,1,0:T(8,128)(2,1)} %param.8) | copy-start | bytes 786436
  0.0 0.8 copy-start.1
  3.8 12.1 %collective-permute-start.3 = (bf16[2,3,128,128]{3,2,1,0:T(8,128)(2,1)S(1)}, bf16[2,3,128,128]{3,2,1,0:T(8,128)(2,1)S(1)}, u32[]{:S(2)}, u32[]{:S(2)}) collective-permute-start(bf16[2,3,128,128]{3,2,1,0:T(8,128)(2,1)S(1)} %get-tuple-element.131), channel_id=1, source_target_pairs={{1,0},{2,1},{3,2},{4,3},{5,4},{6,5},{7,6},{8,7},{9,8},{10,9},{11,1... | collective-permute-start | bytes 589832 | tf_op jit(solution)/shard_map/while/body/eval_jaxpr/ppermute | solution.py:10
  9.3 3.4 %collective-permute-start.2 = (bf16[64,128]{1,0:T(8,128)(2,1)S(1)}, bf16[64,128]{1,0:T(8,128)(2,1)S(1)}, u32[]{:S(2)}, u32[]{:S(2)}) collective-permute-start(bf16[64,128]{1,0:T(8,128)(2,1)S(1)} %get-tuple-element.132), channel_id=1, source_target_pairs={{1,0},{2,1},{3,2},{4,3},{5,4},{6,5},{7,6},{8,7},{9,8},{10,9},{11,1... | collective-permute-start | bytes 49160 | tf_op jit(solution)/shard_map/while/body/eval_jaxpr/ppermute | solution.py:10
  10.0 5.9 %collective-permute-start = (bf16[64,128]{1,0:T(8,128)(2,1)S(1)}, bf16[64,128]{1,0:T(8,128)(2,1)S(1)}, u32[]{:S(2)}, u32[]{:S(2)}) collective-permute-start(bf16[64,128]{1,0:T(8,128)(2,1)S(1)} %get-tuple-element.134), channel_id=1, source_target_pairs={{15,0},{0,1},{1,2},{2,3},{3,4},{4,5},{5,6},{6,7},{7,8},{8,9},{9,10... | collective-permute-start | bytes 49160 | tf_op jit(solution)/shard_map/while/body/eval_jaxpr/ppermute | solution.py:10
  10.0 8.0 %collective-permute-start.1 = (bf16[2,3,128,128]{3,2,1,0:T(8,128)(2,1)S(1)}, bf16[2,3,128,128]{3,2,1,0:T(8,128)(2,1)S(1)}, u32[]{:S(2)}, u32[]{:S(2)}) collective-permute-start(bf16[2,3,128,128]{3,2,1,0:T(8,128)(2,1)S(1)} %get-tuple-element.133), channel_id=1, source_target_pairs={{15,0},{0,1},{1,2},{2,3},{3,4},{4,5},{5,6},{6,7},{7,8},{8,9},{9,10... | collective-permute-start | bytes 589832 | tf_op jit(solution)/shard_map/while/body/eval_jaxpr/ppermute | solution.py:10
  18.9 6.1 %collective-permute-start.3 = (bf16[2,3,128,128]{3,2,1,0:T(8,128)(2,1)S(1)}, bf16[2,3,128,128]{3,2,1,0:T(8,128)(2,1)S(1)}, u32[]{:S(2)}, u32[]{:S(2)}) collective-permute-start(bf16[2,3,128,128]{3,2,1,0:T(8,128)(2,1)S(1)} %get-tuple-element.131), channel_id=1, source_target_pairs={{1,0},{2,1},{3,2},{4,3},{5,4},{6,5},{7,6},{8,7},{9,8},{10,9},{11,1... | collective-permute-start | bytes 589832 | tf_op jit(solution)/shard_map/while/body/eval_jaxpr/ppermute | solution.py:10
  18.9 3.4 %collective-permute-start.2 = (bf16[64,128]{1,0:T(8,128)(2,1)S(1)}, bf16[64,128]{1,0:T(8,128)(2,1)S(1)}, u32[]{:S(2)}, u32[]{:S(2)}) collective-permute-start(bf16[64,128]{1,0:T(8,128)(2,1)S(1)} %get-tuple-element.132), channel_id=1, source_target_pairs={{1,0},{2,1},{3,2},{4,3},{5,4},{6,5},{7,6},{8,7},{9,8},{10,9},{11,1... | collective-permute-start | bytes 49160 | tf_op jit(solution)/shard_map/while/body/eval_jaxpr/ppermute | solution.py:10
  19.1 5.9 %collective-permute-start = (bf16[64,128]{1,0:T(8,128)(2,1)S(1)}, bf16[64,128]{1,0:T(8,128)(2,1)S(1)}, u32[]{:S(2)}, u32[]{:S(2)}) collective-permute-start(bf16[64,128]{1,0:T(8,128)(2,1)S(1)} %get-tuple-element.134), channel_id=1, source_target_pairs={{15,0},{0,1},{1,2},{2,3},{3,4},{4,5},{5,6},{6,7},{7,8},{8,9},{9,10... | collective-permute-start | bytes 49160 | tf_op jit(solution)/shard_map/while/body/eval_jaxpr/ppermute | solution.py:10
  19.4 7.8 %collective-permute-start.1 = (bf16[2,3,128,128]{3,2,1,0:T(8,128)(2,1)S(1)}, bf16[2,3,128,128]{3,2,1,0:T(8,128)(2,1)S(1)}, u32[]{:S(2)}, u32[]{:S(2)}) collective-permute-start(bf16[2,3,128,128]{3,2,1,0:T(8,128)(2,1)S(1)} %get-tuple-element.133), channel_id=1, source_target_pairs={{15,0},{0,1},{1,2},{2,3},{3,4},{4,5},{5,6},{6,7},{7,8},{8,9},{9,10... | collective-permute-start | bytes 589832 | tf_op jit(solution)/shard_map/while/body/eval_jaxpr/ppermute | solution.py:10
  28.2 6.0 %collective-permute-start.3 = (bf16[2,3,128,128]{3,2,1,0:T(8,128)(2,1)S(1)}, bf16[2,3,128,128]{3,2,1,0:T(8,128)(2,1)S(1)}, u32[]{:S(2)}, u32[]{:S(2)}) collective-permute-start(bf16[2,3,128,128]{3,2,1,0:T(8,128)(2,1)S(1)} %get-tuple-element.131), channel_id=1, source_target_pairs={{1,0},{2,1},{3,2},{4,3},{5,4},{6,5},{7,6},{8,7},{9,8},{10,9},{11,1... | collective-permute-start | bytes 589832 | tf_op jit(solution)/shard_map/while/body/eval_jaxpr/ppermute | solution.py:10
  28.2 3.4 %collective-permute-start.2 = (bf16[64,128]{1,0:T(8,128)(2,1)S(1)}, bf16[64,128]{1,0:T(8,128)(2,1)S(1)}, u32[]{:S(2)}, u32[]{:S(2)}) collective-permute-start(bf16[64,128]{1,0:T(8,128)(2,1)S(1)} %get-tuple-element.132), channel_id=1, source_target_pairs={{1,0},{2,1},{3,2},{4,3},{5,4},{6,5},{7,6},{8,7},{9,8},{10,9},{11,1... | collective-permute-start | bytes 49160 | tf_op jit(solution)/shard_map/while/body/eval_jaxpr/ppermute | solution.py:10
  28.2 5.9 %collective-permute-start = (bf16[64,128]{1,0:T(8,128)(2,1)S(1)}, bf16[64,128]{1,0:T(8,128)(2,1)S(1)}, u32[]{:S(2)}, u32[]{:S(2)}) collective-permute-start(bf16[64,128]{1,0:T(8,128)(2,1)S(1)} %get-tuple-element.134), channel_id=1, source_target_pairs={{15,0},{0,1},{1,2},{2,3},{3,4},{4,5},{5,6},{6,7},{7,8},{8,9},{9,10... | collective-permute-start | bytes 49160 | tf_op jit(solution)/shard_map/while/body/eval_jaxpr/ppermute | solution.py:10
  28.7 7.8 %collective-permute-start.1 = (bf16[2,3,128,128]{3,2,1,0:T(8,128)(2,1)S(1)}, bf16[2,3,128,128]{3,2,1,0:T(8,128)(2,1)S(1)}, u32[]{:S(2)}, u32[]{:S(2)}) collective-permute-start(bf16[2,3,128,128]{3,2,1,0:T(8,128)(2,1)S(1)} %get-tuple-element.133), channel_id=1, source_target_pairs={{15,0},{0,1},{1,2},{2,3},{3,4},{4,5},{5,6},{6,7},{7,8},{8,9},{9,10... | collective-permute-start | bytes 589832 | tf_op jit(solution)/shard_map/while/body/eval_jaxpr/ppermute | solution.py:10
  37.4 6.0 %collective-permute-start.3 = (bf16[2,3,128,128]{3,2,1,0:T(8,128)(2,1)S(1)}, bf16[2,3,128,128]{3,2,1,0:T(8,128)(2,1)S(1)}, u32[]{:S(2)}, u32[]{:S(2)}) collective-permute-start(bf16[2,3,128,128]{3,2,1,0:T(8,128)(2,1)S(1)} %get-tuple-element.131), channel_id=1, source_target_pairs={{1,0},{2,1},{3,2},{4,3},{5,4},{6,5},{7,6},{8,7},{9,8},{10,9},{11,1... | collective-permute-start | bytes 589832 | tf_op jit(solution)/shard_map/while/body/eval_jaxpr/ppermute | solution.py:10
  37.4 3.4 %collective-permute-start.2 = (bf16[64,128]{1,0:T(8,128)(2,1)S(1)}, bf16[64,128]{1,0:T(8,128)(2,1)S(1)}, u32[]{:S(2)}, u32[]{:S(2)}) collective-permute-start(bf16[64,128]{1,0:T(8,128)(2,1)S(1)} %get-tuple-element.132), channel_id=1, source_target_pairs={{1,0},{2,1},{3,2},{4,3},{5,4},{6,5},{7,6},{8,7},{9,8},{10,9},{11,1... | collective-permute-start | bytes 49160 | tf_op jit(solution)/shard_map/while/body/eval_jaxpr/ppermute | solution.py:10
  37.5 5.9 %collective-permute-start = (bf16[64,128]{1,0:T(8,128)(2,1)S(1)}, bf16[64,128]{1,0:T(8,128)(2,1)S(1)}, u32[]{:S(2)}, u32[]{:S(2)}) collective-permute-start(bf16[64,128]{1,0:T(8,128)(2,1)S(1)} %get-tuple-element.134), channel_id=1, source_target_pairs={{15,0},{0,1},{1,2},{2,3},{3,4},{4,5},{5,6},{6,7},{7,8},{8,9},{9,10... | collective-permute-start | bytes 49160 | tf_op jit(solution)/shard_map/while/body/eval_jaxpr/ppermute | solution.py:10
  38.0 7.8 %collective-permute-start.1 = (bf16[2,3,128,128]{3,2,1,0:T(8,128)(2,1)S(1)}, bf16[2,3,128,128]{3,2,1,0:T(8,128)(2,1)S(1)}, u32[]{:S(2)}, u32[]{:S(2)}) collective-permute-start(bf16[2,3,128,128]{3,2,1,0:T(8,128)(2,1)S(1)} %get-tuple-element.133), channel_id=1, source_target_pairs={{15,0},{0,1},{1,2},{2,3},{3,4},{4,5},{5,6},{6,7},{7,8},{8,9},{9,10... | collective-permute-start | bytes 589832 | tf_op jit(solution)/shard_map/while/body/eval_jaxpr/ppermute | solution.py:10
  46.7 6.0 %collective-permute-start.3 = (bf16[2,3,128,128]{3,2,1,0:T(8,128)(2,1)S(1)}, bf16[2,3,128,128]{3,2,1,0:T(8,128)(2,1)S(1)}, u32[]{:S(2)}, u32[]{:S(2)}) collective-permute-start(bf16[2,3,128,128]{3,2,1,0:T(8,128)(2,1)S(1)} %get-tuple-element.131), channel_id=1, source_target_pairs={{1,0},{2,1},{3,2},{4,3},{5,4},{6,5},{7,6},{8,7},{9,8},{10,9},{11,1... | collective-permute-start | bytes 589832 | tf_op jit(solution)/shard_map/while/body/eval_jaxpr/ppermute | solution.py:10
  46.7 3.4 %collective-permute-start.2 = (bf16[64,128]{1,0:T(8,128)(2,1)S(1)}, bf16[64,128]{1,0:T(8,128)(2,1)S(1)}, u32[]{:S(2)}, u32[]{:S(2)}) collective-permute-start(bf16[64,128]{1,0:T(8,128)(2,1)S(1)} %get-tuple-element.132), channel_id=1, source_target_pairs={{1,0},{2,1},{3,2},{4,3},{5,4},{6,5},{7,6},{8,7},{9,8},{10,9},{11,1... | collective-permute-start | bytes 49160 | tf_op jit(solution)/shard_map/while/body/eval_jaxpr/ppermute | solution.py:10
  46.7 5.9 %collective-permute-start = (bf16[64,128]{1,0:T(8,128)(2,1)S(1)}, bf16[64,128]{1,0:T(8,128)(2,1)S(1)}, u32[]{:S(2)}, u32[]{:S(2)}) collective-permute-start(bf16[64,128]{1,0:T(8,128)(2,1)S(1)} %get-tuple-element.134), channel_id=1, source_target_pairs={{15,0},{0,1},{1,2},{2,3},{3,4},{4,5},{5,6},{6,7},{7,8},{8,9},{9,10... | collective-permute-start | bytes 49160 | tf_op jit(solution)/shard_map/while/body/eval_jaxpr/ppermute | solution.py:10
  47.2 7.8 %collective-permute-start.1 = (bf16[2,3,128,128]{3,2,1,0:T(8,128)(2,1)S(1)}, bf16[2,3,128,128]{3,2,1,0:T(8,128)(2,1)S(1)}, u32[]{:S(2)}, u32[]{:S(2)}) collective-permute-start(bf16[2,3,128,128]{3,2,1,0:T(8,128)(2,1)S(1)} %get-tuple-element.133), channel_id=1, source_target_pairs={{15,0},{0,1},{1,2},{2,3},{3,4},{4,5},{5,6},{6,7},{7,8},{8,9},{9,10... | collective-permute-start | bytes 589832 | tf_op jit(solution)/shard_map/while/body/eval_jaxpr/ppermute | solution.py:10
  55.9 6.0 %collective-permute-start.3 = (bf16[2,3,128,128]{3,2,1,0:T(8,128)(2,1)S(1)}, bf16[2,3,128,128]{3,2,1,0:T(8,128)(2,1)S(1)}, u32[]{:S(2)}, u32[]{:S(2)}) collective-permute-start(bf16[2,3,128,128]{3,2,1,0:T(8,128)(2,1)S(1)} %get-tuple-element.131), channel_id=1, source_target_pairs={{1,0},{2,1},{3,2},{4,3},{5,4},{6,5},{7,6},{8,7},{9,8},{10,9},{11,1... | collective-permute-start | bytes 589832 | tf_op jit(solution)/shard_map/while/body/eval_jaxpr/ppermute | solution.py:10
  55.9 3.4 %collective-permute-start.2 = (bf16[64,128]{1,0:T(8,128)(2,1)S(1)}, bf16[64,128]{1,0:T(8,128)(2,1)S(1)}, u32[]{:S(2)}, u32[]{:S(2)}) collective-permute-start(bf16[64,128]{1,0:T(8,128)(2,1)S(1)} %get-tuple-element.132), channel_id=1, source_target_pairs={{1,0},{2,1},{3,2},{4,3},{5,4},{6,5},{7,6},{8,7},{9,8},{10,9},{11,1... | collective-permute-start | bytes 49160 | tf_op jit(solution)/shard_map/while/body/eval_jaxpr/ppermute | solution.py:10
  56.0 5.9 %collective-permute-start = (bf16[64,128]{1,0:T(8,128)(2,1)S(1)}, bf16[64,128]{1,0:T(8,128)(2,1)S(1)}, u32[]{:S(2)}, u32[]{:S(2)}) collective-permute-start(bf16[64,128]{1,0:T(8,128)(2,1)S(1)} %get-tuple-element.134), channel_id=1, source_target_pairs={{15,0},{0,1},{1,2},{2,3},{3,4},{4,5},{5,6},{6,7},{7,8},{8,9},{9,10... | collective-permute-start | bytes 49160 | tf_op jit(solution)/shard_map/while/body/eval_jaxpr/ppermute | solution.py:10
  56.5 7.8 %collective-permute-start.1 = (bf16[2,3,128,128]{3,2,1,0:T(8,128)(2,1)S(1)}, bf16[2,3,128,128]{3,2,1,0:T(8,128)(2,1)S(1)}, u32[]{:S(2)}, u32[]{:S(2)}) collective-permute-start(bf16[2,3,128,128]{3,2,1,0:T(8,128)(2,1)S(1)} %get-tuple-element.133), channel_id=1, source_target_pairs={{15,0},{0,1},{1,2},{2,3},{3,4},{4,5},{5,6},{6,7},{7,8},{8,9},{9,10... | collective-permute-start | bytes 589832 | tf_op jit(solution)/shard_map/while/body/eval_jaxpr/ppermute | solution.py:10
  65.2 6.0 %collective-permute-start.3 = (bf16[2,3,128,128]{3,2,1,0:T(8,128)(2,1)S(1)}, bf16[2,3,128,128]{3,2,1,0:T(8,128)(2,1)S(1)}, u32[]{:S(2)}, u32[]{:S(2)}) collective-permute-start(bf16[2,3,128,128]{3,2,1,0:T(8,128)(2,1)S(1)} %get-tuple-element.131), channel_id=1, source_target_pairs={{1,0},{2,1},{3,2},{4,3},{5,4},{6,5},{7,6},{8,7},{9,8},{10,9},{11,1... | collective-permute-start | bytes 589832 | tf_op jit(solution)/shard_map/while/body/eval_jaxpr/ppermute | solution.py:10
  65.2 3.4 %collective-permute-start.2 = (bf16[64,128]{1,0:T(8,128)(2,1)S(1)}, bf16[64,128]{1,0:T(8,128)(2,1)S(1)}, u32[]{:S(2)}, u32[]{:S(2)}) collective-permute-start(bf16[64,128]{1,0:T(8,128)(2,1)S(1)} %get-tuple-element.132), channel_id=1, source_target_pairs={{1,0},{2,1},{3,2},{4,3},{5,4},{6,5},{7,6},{8,7},{9,8},{10,9},{11,1... | collective-permute-start | bytes 49160 | tf_op jit(solution)/shard_map/while/body/eval_jaxpr/ppermute | solution.py:10
  65.2 5.9 %collective-permute-start = (bf16[64,128]{1,0:T(8,128)(2,1)S(1)}, bf16[64,128]{1,0:T(8,128)(2,1)S(1)}, u32[]{:S(2)}, u32[]{:S(2)}) collective-permute-start(bf16[64,128]{1,0:T(8,128)(2,1)S(1)} %get-tuple-element.134), channel_id=1, source_target_pairs={{15,0},{0,1},{1,2},{2,3},{3,4},{4,5},{5,6},{6,7},{7,8},{8,9},{9,10... | collective-permute-start | bytes 49160 | tf_op jit(solution)/shard_map/while/body/eval_jaxpr/ppermute | solution.py:10
  65.7 7.8 %collective-permute-start.1 = (bf16[2,3,128,128]{3,2,1,0:T(8,128)(2,1)S(1)}, bf16[2,3,128,128]{3,2,1,0:T(8,128)(2,1)S(1)}, u32[]{:S(2)}, u32[]{:S(2)}) collective-permute-start(bf16[2,3,128,128]{3,2,1,0:T(8,128)(2,1)S(1)} %get-tuple-element.133), channel_id=1, source_target_pairs={{15,0},{0,1},{1,2},{2,3},{3,4},{4,5},{5,6},{6,7},{7,8},{8,9},{9,10... | collective-permute-start | bytes 589832 | tf_op jit(solution)/shard_map/while/body/eval_jaxpr/ppermute | solution.py:10
  74.4 3.2 %collective-permute-start.5 = (bf16[2,3,128,128]{3,2,1,0:T(8,128)(2,1)S(1)}, bf16[2,3,128,128]{3,2,1,0:T(8,128)(2,1)S(1)}, u32[]{:S(2)}, u32[]{:S(2)}) collective-permute-start(bf16[2,3,128,128]{3,2,1,0:T(8,128)(2,1)S(1)} %get-tuple-element.52), channel_id=1, source_target_pairs={{1,0},{2,1},{3,2},{4,3},{5,4},{6,5},{7,6},{8,7},{9,8},{10,9},{11,1... | collective-permute-start | bytes 589832 | tf_op jit(solution)/shard_map/ppermute | solution.py:10
  74.5 3.6 %collective-permute-start.4 = (bf16[64,128]{1,0:T(8,128)(2,1)S(1)}, bf16[64,128]{1,0:T(8,128)(2,1)S(1)}, u32[]{:S(2)}, u32[]{:S(2)}) collective-permute-start(bf16[64,128]{1,0:T(8,128)(2,1)S(1)} %get-tuple-element.51), channel_id=1, source_target_pairs={{1,0},{2,1},{3,2},{4,3},{5,4},{6,5},{7,6},{8,7},{9,8},{10,9},{11,1... | collective-permute-start | bytes 49160 | tf_op jit(solution)/shard_map/ppermute | solution.py:10
where the time goes:
time: 79.1 us; the launch traced here: 78.9 us
  waiting for transfers between devices  46 us (58%)
  starting transfers between devices  19.9 us (25%)
  matrix products  9.13 us (12%)
  local copies, waits for them, and re-layouts  3.32 us (4%)
    ppermute x30, waiting for transfers between devices, passed_along(): return lax.ppermute(block, axis, route)  46 us
    ppermute x30, starting transfers between devices, passed_along(): return lax.ppermute(block, axis, route)  19.9 us
    dot_general x16, matrix products, token_pair_function(): jnp.einsum('qun,qpn->qup', local_token_block[0], passing_block[0], prefer...  3.36 us
    dot_general x16, matrix products, token_pair_function(): jnp.einsum('qun,qpn->qup', local_token_block[1], passing_block[1], prefer...  3.04 us
    dot_general x16, matrix products, rows_term(): lax.dot_general(visitor_queries, kernel, (((1,), (1,)), ((), ())), prefer...  2.73 us
  transfers between devices with their start and end apart: 30, of which 22 were waited for; matrix products, arithmetic and copies ran while one was open for 2% of the time, Pallas kernels for 0%

commit v1 on v0

v1 whole, which is shorter than its diff:
```python
import functools

import jax
import jax.numpy as jnp
from jax import lax
from jax.experimental import pallas as pl
from jax.experimental.pallas import tpu as pltpu
from jax.sharding import PartitionSpec as P

MESH = pl.DeviceIdType.MESH
RETURN_TYPE = jnp.bfloat16


def passed_along(block, axis, distance):
    devices = range(lax.axis_size(axis))
    route = [((i - distance) % len(devices), i) for i in devices]
    return lax.ppermute(block, axis, route)


def token_pair_function(local_token_block, passing_block):
    input_product_matrix = jnp.einsum(
        "qun,qpn->qup", local_token_block[0], passing_block[0], preferred_element_type=jnp.float32
    )
    grad_gram = jnp.einsum(
        "qun,qpn->qup", local_token_block[1], passing_block[1], preferred_element_type=jnp.float32
    )
    return jnp.sum(input_product_matrix * grad_gram, axis=0).astype(jnp.bfloat16)


def rows_term(kernel, visitor_queries):
    return lax.dot_general(
        visitor_queries, kernel, (((1,), (1,)), ((), ())), preferred_element_type=jnp.float32
    )


def one_way_ring(activations, gradients, queries, layer_ids):
    own = jnp.stack(
        [jnp.take(activations, layer_ids, axis=0), jnp.take(gradients, layer_ids, axis=0)]
    )
    influence = rows_term(token_pair_function(own, own), queries)

    def turn(_, carried_state):
        result, block, visitor_queries = carried_state
        block = passed_along(block, "tok", 1)
        visitor_queries = passed_along(visitor_queries, "tok", 1)
        result = result + rows_term(token_pair_function(own, block), visitor_queries)
        return result, block, visitor_queries

    steps = lax.axis_size("tok") - 1
    return lax.fori_loop(0, steps, turn, (influence, own, queries))[0]


def window_kernel(
    n, snake, ids, acts, grads, queries, out, data, qs, total, back, came, send, recv, bsend, brecv
):
    chips = n // 2
    reach = chips // 4
    layers = ids.shape[0]
    pieces = layers + 1
    me = lax.axis_index("tok")
    core = lax.rem(me, 2)
    chip = lax.div(me, 2)
    if snake:
        place = jnp.where(lax.rem(chip, 2) == 0, lax.div(chip, 2), chips - 1 - lax.div(chip, 2))
    else:
        place = chip

    def device_at(step):
        to = lax.rem(place + step + chips, chips)
        if snake:
            to = jnp.where(to < chips // 2, 2 * to, 2 * (chips - 1 - to) + 1)
        return {"tok": 2 * to + core}

    other = {"tok": 2 * chip + 1 - core}

    barrier = pltpu.get_barrier_semaphore()
    for step in range(1, reach + 1):
        for sign in (1, -1):
            pl.semaphore_signal(barrier, inc=1, device_id=device_at(sign * step), device_id_type=MESH)
    pl.semaphore_signal(barrier, inc=1, device_id=other, device_id_type=MESH)

    for l in range(layers):
        data[reach, 0, l, 0] = acts[ids[l]]
        data[reach, 0, l, 1] = grads[ids[l]]
    qs[reach, 0] = queries[...]
    pl.semaphore_wait(barrier, 2 * reach + 1)

    started = []

    def part(o, m, piece):
        return data.at[reach + o, m, piece] if piece < layers else qs.at[reach + o, m]

    def copy_of(way, o, to_o, to_m, piece, device):
        return pltpu.make_async_remote_copy(
            src_ref=part(o, 0, piece),
            dst_ref=part(to_o, to_m, piece),
            send_sem=send.at[way, reach + o, piece],
            recv_sem=recv.at[reach + to_o, to_m, piece],
            device_id=device,
            device_id_type=MESH,
        )

    ahead, behind = device_at(1), device_at(-1)

    def pass_on(o, piece):
        if -reach < o <= 0:
            started.append(copy_of(0, o, o - 1, 0, piece, ahead))
            started[-1].start()
        if 0 <= o < reach:
            started.append(copy_of(1, o, o + 1, 0, piece, behind))
            started[-1].start()
        started.append(copy_of(2, o, o, 1, piece, other))
        started[-1].start()

    def arrived(o, m, piece):
        if m == 1:
            copy_of(2, o, o, 1, piece, other).wait_recv()
        elif o < 0:
            copy_of(0, o + 1, o, 0, piece, ahead).wait_recv()
        else:
            copy_of(1, o - 1, o, 0, piece, behind).wait_recv()

    def term(target, source):
        kernel = None
        for l in range(layers):
            product = None
            for kind in range(2):
                rows = data[source, :, l, kind]
                rows = rows.reshape(rows.shape[0] * rows.shape[1], rows.shape[2])
                gram = lax.dot_general(
                    rows, data[target, 0, l, kind], (((1,), (1,)), ((), ())),
                    preferred_element_type=jnp.float32,
                )
                product = gram if product is None else product * gram
            kernel = product if kernel is None else kernel + product
        kernel = kernel.astype(jnp.bfloat16)
        tokens = kernel.shape[0] // 2
        return jnp.dot(
            qs[source, 0], kernel[:tokens], preferred_element_type=jnp.float32
        ) + jnp.dot(qs[source, 1], kernel[tokens:], preferred_element_type=jnp.float32)

    for piece in range(pieces):
        pass_on(0, piece)
    for j in range(1, reach + 1):
        for piece in range(pieces):
            for o in (-j, j):
                arrived(o, 0, piece)
                pass_on(o, piece)
        if j == 1:
            for piece in range(pieces):
                arrived(0, 1, piece)
            total[...] = term(reach, reach)
        for piece in range(pieces):
            for o in (-j, j):
                arrived(o, 1, piece)
        if j < reach:
            for o in (-j, j):
                total[...] += term(reach, reach + o)

    work = [(2 * reach - 2, jnp.where(core == 0, -reach, reach), jnp.where(core == 0, 2 * reach, 0))]
    for j in range(reach - 1, 0, -1):
        work.append((2 * j - 2, -j, 2 * reach))
        work.append((2 * j - 1, j, 0))

    def back_copy(slot, step):
        return pltpu.make_async_remote_copy(
            src_ref=back.at[slot],
            dst_ref=came.at[slot],
            send_sem=bsend.at[slot],
            recv_sem=brecv.at[slot],
            device_id=device_at(step),
            device_id_type=MESH,
        )

    waiting = None
    for slot, target, source in work:
        back[slot] = term(reach + target, source).astype(back.dtype)
        if waiting is not None:
            started.append(back_copy(*waiting))
            started[-1].start()
        waiting = (slot, target)
    total[...] += term(reach, 0)
    started.append(back_copy(*waiting))
    started[-1].start()
    total[...] += term(reach, 2 * reach)
    result = total[...]
    for slot, target, _ in work:
        back_copy(slot, target).wait_recv()
        result = result + came[slot].astype(jnp.float32)
    out[...] = result
    for copy in started:
        copy.wait_send()


def windows(n, snake, activations, gradients, queries, layer_ids):
    layers = layer_ids.shape[0]
    tokens, width = activations.shape[1:]
    reach = n // 8
    slots = 2 * reach + 1
    vmem = pl.BlockSpec(memory_space=pltpu.VMEM)
    return pl.pallas_call(
        functools.partial(window_kernel, n, snake),
        out_shape=jax.ShapeDtypeStruct(queries.shape, jnp.float32),
        in_specs=[pl.BlockSpec(memory_space=pltpu.SMEM), vmem, vmem, vmem],
        out_specs=vmem,
        scratch_shapes=[
            pltpu.VMEM((slots, 2, layers, 2, tokens, width), activations.dtype),
            pltpu.VMEM((slots, 2) + queries.shape, queries.dtype),
            pltpu.VMEM(queries.shape, jnp.float32),
            pltpu.VMEM((2 * reach - 1,) + queries.shape, RETURN_TYPE),
            pltpu.VMEM((2 * reach - 1,) + queries.shape, RETURN_TYPE),
            pltpu.SemaphoreType.DMA((3, slots, layers + 1)),
            pltpu.SemaphoreType.DMA((slots, 2, layers + 1)),
            pltpu.SemaphoreType.DMA((2 * reach - 1,)),
            pltpu.SemaphoreType.DMA((2 * reach - 1,)),
        ],
        compiler_params=pltpu.CompilerParams(collective_id=0, has_side_effects=True),
    )(layer_ids, activations, gradients, queries)


def longest_step(chips):
    steps = zip(chips, chips[1:] + chips[:1])
    return max(sum(abs(a - b) for a, b in zip(p, q)) for p, q in steps)


def solution(mesh):
    n = mesh.shape["tok"]
    if n % 8 == 0:
        devices = mesh.devices[0]
        snake = False
        if hasattr(devices[0], "coords"):
            chips = [tuple(d.coords) for d in devices[::2]]
            snake = longest_step(chips[::2] + chips[::-1][::2]) < longest_step(chips)
        body = functools.partial(windows, n, snake)
    else:
        body = one_way_ring
    return jax.shard_map(
        body,
        mesh=mesh,
        in_specs=(
            P(None, ("groups", "tok"), None),
            P(None, ("groups", "tok"), None),
            P(None, ("groups", "tok")),
            P(),
        ),
        out_specs=P(None, ("groups", "tok")),
        check_vma=False,
    )
```

time: 79.1 us -> 23.9 us (0.30)
  waiting for transfers between devices: 46 us -> 0 us
  Pallas kernels: 0 us -> 22.3 us
  starting transfers between devices: 19.9 us -> 0 us
  matrix products: 9.13 us -> 0 us
  local copies, waits for them, and re-layouts: 3.32 us -> 1.38 us
    ppermute x30 -> x0, waiting for transfers between devices: 46 us -> none  [passed_along(): return lax.ppermute(block, axis, route)]
    pallas_call x0 -> x1, Pallas kernels: none -> 22.3 us  [windows(): pl.pallas_call(functools.partial(window_kernel, n, snake), out_shape=jax....]
    ppermute x30 -> x0, starting transfers between devices: 19.9 us -> none  [passed_along(): return lax.ppermute(block, axis, route)]
    dot_general x48 -> x0, matrix products: 9.13 us -> none  [the longest x16 3.36 us: token_pair_function(): jnp.einsum('qun,qpn->qup', local_token_block[0], passing_block[0], prefer...]
    gather x2 -> x0, local copies, waits for them, and re-layouts: 2.08 us -> none  [the longest x1 1.52 us: body(): jnp.take(gradients, layer_ids, axis=0)]
  transfers between devices with their start and end apart: 30 -> 0, of which waited for: 22 -> 0; matrix products, arithmetic and copies ran while one was open for 2% -> 0% of each run, Pallas kernels for 0% -> 0%
where the time goes in v1:
time: 23.9 us; the launch traced here: 23.7 us
  Pallas kernels  22.3 us (93%)
  local copies, waits for them, and re-layouts  1.38 us (6%)
    pallas_call x1, Pallas kernels, windows(): pl.pallas_call(functools.partial(window_kernel, n, snake), out_shape=jax....  22.3 us
    unnamed x1, local copies, waits for them, and re-layouts  1.38 us

profile of v1, /device:TPU:0, one launch (start us, length us, event | category | flops | bytes accessed | tf_op | source)
XLA Modules:
  0.0 23.7 jit_solution(10630925973339985808)
XLA Ops:
  0.0 22.3 %shard_map.46 = f32[64,128]{1,0:T(8,128)} custom-call(s32[3]{0:T(128)} %ids.1, bf16[8,128,128]{2,1,0:T(8,128)(2,1)} %acts.1, bf16[8,128,128]{2,1,0:T(8,128)(2,1)} %grads.1, bf16[64,128]{1,0:T(8,128)(2,1)} %queries.1), custom_call_target="tpu_custom_call" | custom-call | tf_op jit(solution)/shard_map/pallas_call | solution.py:201
  22.3 1.4 %copy.6 = f32[64,128]{1,0:T(8,128)} copy(f32[64,128]{1,0:T(8,128)} %shard_map.46) | data formatting | bytes 65536

commit v2 on v1

--- a/solution.py
+++ b/solution.py
@@ -51,7 +51,7 @@
 
 
 def window_kernel(
-    n, snake, ids, acts, grads, queries, out, data, qs, total, back, came, send, recv, bsend, brecv
+    n, snake, ids, acts, grads, queries, out, stored, data, qs, total, back, came, load, send, recv, bsend, brecv
 ):
     chips = n // 2
     reach = chips // 4
@@ -74,16 +74,23 @@
     other = {"tok": 2 * chip + 1 - core}
 
     barrier = pltpu.get_barrier_semaphore()
-    for step in range(1, reach + 1):
-        for sign in (1, -1):
-            pl.semaphore_signal(barrier, inc=1, device_id=device_at(sign * step), device_id_type=MESH)
+    for sign in (1, -1):
+        pl.semaphore_signal(barrier, inc=1, device_id=device_at(sign), device_id_type=MESH)
     pl.semaphore_signal(barrier, inc=1, device_id=other, device_id_type=MESH)
 
+    loads = [
+        pltpu.make_async_copy(queries, qs.at[reach, 0], load.at[0]),
+        pltpu.make_async_copy(acts, stored.at[0], load.at[1]),
+        pltpu.make_async_copy(grads, stored.at[1], load.at[2]),
+    ]
+    for copy in loads:
+        copy.start()
+    for copy in loads:
+        copy.wait()
     for l in range(layers):
-        data[reach, 0, l, 0] = acts[ids[l]]
-        data[reach, 0, l, 1] = grads[ids[l]]
-    qs[reach, 0] = queries[...]
-    pl.semaphore_wait(barrier, 2 * reach + 1)
+        for kind in range(2):
+            data[reach, 0, l, kind] = stored[kind, ids[l]]
+    pl.semaphore_wait(barrier, 3)
 
     started = []
 
@@ -201,14 +208,16 @@
     return pl.pallas_call(
         functools.partial(window_kernel, n, snake),
         out_shape=jax.ShapeDtypeStruct(queries.shape, jnp.float32),
-        in_specs=[pl.BlockSpec(memory_space=pltpu.SMEM), vmem, vmem, vmem],
+        in_specs=[pl.BlockSpec(memory_space=pltpu.SMEM)] + [pl.BlockSpec(memory_space=pl.ANY)] * 3,
         out_specs=vmem,
         scratch_shapes=[
+            pltpu.VMEM((2,) + activations.shape, activations.dtype),
             pltpu.VMEM((slots, 2, layers, 2, tokens, width), activations.dtype),
             pltpu.VMEM((slots, 2) + queries.shape, queries.dtype),
             pltpu.VMEM(queries.shape, jnp.float32),
             pltpu.VMEM((2 * reach - 1,) + queries.shape, RETURN_TYPE),
             pltpu.VMEM((2 * reach - 1,) + queries.shape, RETURN_TYPE),
+            pltpu.SemaphoreType.DMA((3,)),
             pltpu.SemaphoreType.DMA((3, slots, layers + 1)),
             pltpu.SemaphoreType.DMA((slots, 2, layers + 1)),
             pltpu.SemaphoreType.DMA((2 * reach - 1,)),

time: 23.9 us -> 23.1 us (0.967)
  Pallas kernels: 22.3 us -> 21.5 us
    pallas_call x1, Pallas kernels: 22.3 us -> 21.5 us  [windows(): pl.pallas_call(functools.partial(window_kernel, n, snake), out_shape=jax....]
where the time goes in v2:
time: 23.1 us; the launch traced here: 22.8 us
  Pallas kernels  21.5 us (93%)
  local copies, waits for them, and re-layouts  1.38 us (6%)
    pallas_call x1, Pallas kernels, windows(): pl.pallas_call(functools.partial(window_kernel, n, snake), out_shape=jax....  21.5 us
    unnamed x1, local copies, waits for them, and re-layouts  1.38 us

profile of v2, /device:TPU:0, one launch (start us, length us, event | category | flops | bytes accessed | tf_op | source)
XLA Modules:
  0.0 22.8 jit_solution(6616728043727126964)
XLA Ops:
  0.0 21.5 %shard_map.46 = f32[64,128]{1,0:T(8,128)} custom-call(s32[3]{0:T(128)} %ids.1, bf16[8,128,128]{2,1,0:T(8,128)(2,1)} %acts.1, bf16[8,128,128]{2,1,0:T(8,128)(2,1)} %grads.1, bf16[64,128]{1,0:T(8,128)(2,1)} %queries.1), custom_call_target="tpu_custom_call" | custom-call | tf_op jit(solution)/shard_map/pallas_call | solution.py:208
  21.5 1.4 %copy.6 = f32[64,128]{1,0:T(8,128)} copy(f32[64,128]{1,0:T(8,128)} %shard_map.46) | data formatting | bytes 65536

commit v3 on v2

--- a/solution.py
+++ b/solution.py
@@ -207,7 +207,7 @@
     vmem = pl.BlockSpec(memory_space=pltpu.VMEM)
     return pl.pallas_call(
         functools.partial(window_kernel, n, snake),
-        out_shape=jax.ShapeDtypeStruct(queries.shape, jnp.float32),
+        out_shape=pltpu.VMEM(queries.shape, jnp.float32),
         in_specs=[pl.BlockSpec(memory_space=pltpu.SMEM)] + [pl.BlockSpec(memory_space=pl.ANY)] * 3,
         out_specs=vmem,
         scratch_shapes=[

time: 23.1 us -> 21.7 us (0.939)
  local copies, waits for them, and re-layouts: 1.38 us -> 0.62 us
  Pallas kernels: 21.5 us -> 20.9 us
    unnamed x1, local copies, waits for them, and re-layouts: 1.38 us -> 0.62 us
    pallas_call x1, Pallas kernels: 21.5 us -> 20.9 us  [windows(): pl.pallas_call(functools.partial(window_kernel, n, snake), out_shape=pltp...]
where the time goes in v3:
time: 21.7 us; the launch traced here: 21.5 us
  Pallas kernels  20.9 us (96%)
  local copies, waits for them, and re-layouts  0.62 us (3%)
    pallas_call x1, Pallas kernels, windows(): pl.pallas_call(functools.partial(window_kernel, n, snake), out_shape=pltp...  20.9 us
    unnamed x1, local copies, waits for them, and re-layouts  0.62 us

profile of v3, /device:TPU:0, one launch (start us, length us, event | category | flops | bytes accessed | tf_op | source)
XLA Modules:
  0.0 21.5 jit_solution(1950961818558755600)
XLA Ops:
  0.0 20.9 %shard_map.46 = f32[64,128]{1,0:T(8,128)S(1)} custom-call(s32[3]{0:T(128)} %ids.1, bf16[8,128,128]{2,1,0:T(8,128)(2,1)} %acts.1, bf16[8,128,128]{2,1,0:T(8,128)(2,1)} %grads.1, bf16[64,128]{1,0:T(8,128)(2,1)} %queries.1), custom_call_target="tpu_custom_call" | custom-call | tf_op jit(solution)/shard_map/pallas_call | solution.py:208
  20.9 0.6 %copy.6 = f32[64,128]{1,0:T(8,128)} copy(f32[64,128]{1,0:T(8,128)S(1)} %shard_map.46) | data formatting | bytes 65536

commit v4 on v3

--- a/solution.py
+++ b/solution.py
@@ -51,7 +51,7 @@
 
 
 def window_kernel(
-    n, snake, ids, acts, grads, queries, out, stored, data, qs, total, back, came, load, send, recv, bsend, brecv
+    n, snake, layer_ids, acts, grads, queries, out, ids, stored, data, qs, total, back, came, load, send, recv, bsend, brecv
 ):
     chips = n // 2
     reach = chips // 4
@@ -82,6 +82,7 @@
         pltpu.make_async_copy(queries, qs.at[reach, 0], load.at[0]),
         pltpu.make_async_copy(acts, stored.at[0], load.at[1]),
         pltpu.make_async_copy(grads, stored.at[1], load.at[2]),
+        pltpu.make_async_copy(layer_ids, ids, load.at[3]),
     ]
     for copy in loads:
         copy.start()
@@ -109,6 +110,10 @@
 
     ahead, behind = device_at(1), device_at(-1)
 
+    def share(o, piece):
+        started.append(copy_of(2, o, o, 1, piece, other))
+        started[-1].start()
+
     def pass_on(o, piece):
         if -reach < o <= 0:
             started.append(copy_of(0, o, o - 1, 0, piece, ahead))
@@ -116,8 +121,8 @@
         if 0 <= o < reach:
             started.append(copy_of(1, o, o + 1, 0, piece, behind))
             started[-1].start()
-        started.append(copy_of(2, o, o, 1, piece, other))
-        started[-1].start()
+        if o:
+            share(o, piece)
 
     def arrived(o, m, piece):
         if m == 1:
@@ -148,6 +153,8 @@
 
     for piece in range(pieces):
         pass_on(0, piece)
+    for piece in range(pieces):
+        share(0, piece)
     for j in range(1, reach + 1):
         for piece in range(pieces):
             for o in (-j, j):
@@ -208,16 +215,17 @@
     return pl.pallas_call(
         functools.partial(window_kernel, n, snake),
         out_shape=pltpu.VMEM(queries.shape, jnp.float32),
-        in_specs=[pl.BlockSpec(memory_space=pltpu.SMEM)] + [pl.BlockSpec(memory_space=pl.ANY)] * 3,
+        in_specs=[pl.BlockSpec(memory_space=pl.ANY)] * 4,
         out_specs=vmem,
         scratch_shapes=[
+            pltpu.SMEM(layer_ids.shape, layer_ids.dtype),
             pltpu.VMEM((2,) + activations.shape, activations.dtype),
             pltpu.VMEM((slots, 2, layers, 2, tokens, width), activations.dtype),
             pltpu.VMEM((slots, 2) + queries.shape, queries.dtype),
             pltpu.VMEM(queries.shape, jnp.float32),
             pltpu.VMEM((2 * reach - 1,) + queries.shape, RETURN_TYPE),
             pltpu.VMEM((2 * reach - 1,) + queries.shape, RETURN_TYPE),
-            pltpu.SemaphoreType.DMA((3,)),
+            pltpu.SemaphoreType.DMA((4,)),
             pltpu.SemaphoreType.DMA((3, slots, layers + 1)),
             pltpu.SemaphoreType.DMA((slots, 2, layers + 1)),
             pltpu.SemaphoreType.DMA((2 * reach - 1,)),

time: 21.7 us -> 21 us (0.968)
  Pallas kernels: 20.9 us -> 20.2 us
    pallas_call x1, Pallas kernels: 20.9 us -> 20.2 us  [windows(): pl.pallas_call(functools.partial(window_kernel, n, snake), out_shape=pltp...]
where the time goes in v4:
time: 21 us; the launch traced here: 20.8 us
  Pallas kernels  20.2 us (96%)
  local copies, waits for them, and re-layouts  0.62 us (3%)
    pallas_call x1, Pallas kernels, windows(): pl.pallas_call(functools.partial(window_kernel, n, snake), out_shape=pltp...  20.2 us
    unnamed x1, local copies, waits for them, and re-layouts  0.62 us

profile of v4, /device:TPU:0, one launch (start us, length us, event | category | flops | bytes accessed | tf_op | source)
XLA Modules:
  0.0 20.8 jit_solution(12948769321525428633)
XLA Ops:
  0.0 20.2 %shard_map.46 = f32[64,128]{1,0:T(8,128)S(1)} custom-call(s32[3]{0:T(128)} %layer_ids.1, bf16[8,128,128]{2,1,0:T(8,128)(2,1)} %acts.1, bf16[8,128,128]{2,1,0:T(8,128)(2,1)} %grads.1, bf16[64,128]{1,0:T(8,128)(2,1)} %queries.1), custom_call_target="tpu_custom_call" | custom-call | tf_op jit(solution)/shard_map/pallas_call | solution.py:215
  20.2 0.6 %copy.6 = f32[64,128]{1,0:T(8,128)} copy(f32[64,128]{1,0:T(8,128)S(1)} %shard_map.46) | data formatting | bytes 65536

commit v5 on v4

--- a/solution.py
+++ b/solution.py
@@ -140,16 +140,13 @@
                 rows = data[source, :, l, kind]
                 rows = rows.reshape(rows.shape[0] * rows.shape[1], rows.shape[2])
                 gram = lax.dot_general(
-                    rows, data[target, 0, l, kind], (((1,), (1,)), ((), ())),
+                    data[target, 0, l, kind], rows, (((1,), (1,)), ((), ())),
                     preferred_element_type=jnp.float32,
                 )
                 product = gram if product is None else product * gram
             kernel = product if kernel is None else kernel + product
-        kernel = kernel.astype(jnp.bfloat16)
-        tokens = kernel.shape[0] // 2
-        return jnp.dot(
-            qs[source, 0], kernel[:tokens], preferred_element_type=jnp.float32
-        ) + jnp.dot(qs[source, 1], kernel[tokens:], preferred_element_type=jnp.float32)
+        visitor_queries = jnp.concatenate([qs[source, 0], qs[source, 1]], axis=1)
+        return rows_term(kernel.astype(jnp.bfloat16), visitor_queries)
 
     for piece in range(pieces):
         pass_on(0, piece)

time: 21 us -> 21 us (level)
  no operation moved by 1% of the time
where the time goes in v5:
time: 21 us; the launch traced here: 20.8 us
  Pallas kernels  20.1 us (96%)
  local copies, waits for them, and re-layouts  0.62 us (3%)
    pallas_call x1, Pallas kernels, windows(): pl.pallas_call(functools.partial(window_kernel, n, snake), out_shape=pltp...  20.1 us
    unnamed x1, local copies, waits for them, and re-layouts  0.62 us

profile of v5, /device:TPU:0, one launch (start us, length us, event | category | flops | bytes accessed | tf_op | source)
XLA Modules:
  0.0 20.8 jit_solution(8016594506506482789)
XLA Ops:
  0.0 20.1 %shard_map.46 = f32[64,128]{1,0:T(8,128)S(1)} custom-call(s32[3]{0:T(128)} %layer_ids.1, bf16[8,128,128]{2,1,0:T(8,128)(2,1)} %acts.1, bf16[8,128,128]{2,1,0:T(8,128)(2,1)} %grads.1, bf16[64,128]{1,0:T(8,128)(2,1)} %queries.1), custom_call_target="tpu_custom_call" | custom-call | tf_op jit(solution)/shard_map/pallas_call | solution.py:212
  20.1 0.6 %copy.6 = f32[64,128]{1,0:T(8,128)} copy(f32[64,128]{1,0:T(8,128)S(1)} %shard_map.46) | data formatting | bytes 65536
